TPU v7x, 512 devices: a whole 4x4x16 slice. The times are simulated.
512 devices in a mesh: row: 16 (over y, x), col: 32 (over z, core).
Axes of the slice: x: 4, y: 4, z: 16, core: 2. Of those that a mesh axis runs over, the one named last changes fastest.
Arguments:
- out_grad: bfloat16 [2048, 8192], P('col', 'row'), may hold values from -6 to 6
- hidden: bfloat16 [2048, 28672], P('row', 'col'), may hold values from -0.12988281 to 0.12988281
- weight: bfloat16 [28672, 8192], P('col', 'row'), may hold values from -0.03125 to 0.03125
Outputs:
- token_grad: bfloat16 [2048, 28672], P('row', 'col')
- weight_grad: bfloat16 [28672, 8192], P('col', 'row')
All inputs are finite; a program needn't handle non-finite values.
Results may differ from a plain program's by a relative error of at most 0.001.
Values may be sent and summed in bfloat16 or wider, within the bound.
A program may use at most 64 MiB of HBM per device.

v0:
```python
import jax
import jax.numpy as jnp
from jax import lax
from jax.sharding import PartitionSpec as P


def on_device(out_grad, hidden, weight):
    gathered = lax.all_gather(out_grad, "col", axis=0, tiled=True)
    cotangent = gathered
    weight_sum = lax.dot_general(
        lax.all_gather(hidden, "row", axis=0, tiled=True),
        cotangent,
        (((0,), (0,)), ((), ())),
        preferred_element_type=jnp.float32,
    )
    weight_grad = weight_sum.astype(jnp.bfloat16)
    own_full = lax.all_to_all(gathered, "row", split_axis=0, concat_axis=1, tiled=True)
    cotangent = own_full
    token_sum = lax.dot_general(
        cotangent,
        lax.all_gather(weight, "row", axis=1, tiled=True),
        (((1,), (1,)), ((), ())),
        preferred_element_type=jnp.float32,
    )
    return (token_sum.astype(jnp.bfloat16), weight_grad)


def solution(mesh):
    return jax.shard_map(
        on_device,
        mesh=mesh,
        in_specs=(P("col", "row"), P("row", "col"), P("col", "row")),
        out_specs=(P("row", "col"), P("col", "row")),
        check_vma=False,
    )
```

profile of v0, /device:TPU:1, one launch (start us, length us, event | category | flops | bytes accessed | tf_op | source)
XLA Modules:
  0.0 301.2 jit_solution(12447496459693819890)
XLA Ops:
  7.2 0.0 all-gather.4.cloned.1.call-start
  7.2 0.7 all-gather.4.cloned.1.call-update
  7.9 0.0 all-gather.8.cloned.1.call-start
  7.9 0.7 all-gather.8.cloned.1.call-update
  8.6 0.0 all-gather.6.cloned.1.call-start
  8.7 0.7 all-gather.6.cloned.1.call-update
  9.4 78.3 %all-gather.4.cloned.1.call-done = bf16[2048,512]{1,0:T(8,128)(2,1)} async-done(((bf16[64,512]{1,0:T(8,128)(2,1)}), bf16[2048,512]{1,0:T(8,128)(2,1)}) %all-gather.4.cloned.1.call-update) | async-done | bytes 2097168 | tf_op jit(solution)/shard_map/all_gather | solution.py:8
  87.7 37.9 %all_to_all.19 = bf16[16,128,512]{2,1,0:T(8,128)(2,1)S(1)} all-to-all(bf16[16,128,512]{2,1,0:T(8,128)(2,1)} %bitcast.9), channel_id=1, replica_groups=mesh['row'=16,'col'=32] {'row'}, dimensions={0} | all-to-all | bytes 4194304 | tf_op jit(solution)/shard_map/all_to_all | solution.py:17
  125.6 2.4 copy.5
  127.9 0.0 copy-start
  127.9 28.6 %all-gather.8.cloned.1.call-done = bf16[2048,896]{1,0:T(8,128)(2,1)} async-done(((bf16[128,896]{1,0:T(8,128)(2,1)}), bf16[2048,896]{1,0:T(8,128)(2,1)}) %all-gather.8.cloned.1.call-update) | async-done | bytes 3670032 | tf_op jit(solution)/shard_map/all_gather | solution.py:11
  156.6 5.7 %convolution_convert_fusion = bf16[896,512]{1,0:T(8,128)(2,1)} fusion(bf16[2048,896]{1,0:T(8,128)(2,1)} %all-gather.8.cloned.1.call-done, bf16[2048,512]{1,0:T(8,128)(2,1)} %all-gather.4.cloned.1.call-done), kind=kOutput, calls=%fused_computation | convolution fusion | flops 1879506944 | bytes 6684672 | tf_op jit(solution)/shard_map/dot_general | solution.py:10
  162.3 121.8 %all-gather.6.cloned.1.call-done = bf16[896,8192]{1,0:T(8,128)(2,1)} async-done(((bf16[896,512]{1,0:T(8,128)(2,1)}), bf16[896,8192]{1,0:T(8,128)(2,1)}) %all-gather.6.cloned.1.call-update) | async-done | bytes 14680080 | tf_op jit(solution)/shard_map/all_gather | solution.py:21
  284.1 0.0 copy-done
  284.1 10.6 %convolution_convert_fusion.1 = bf16[128,896]{1,0:T(8,128)(2,1)} fusion(bf16[128,8192]{0,1:T(8,128)(2,1)S(1)} %bitcast.8, bf16[896,8192]{1,0:T(8,128)(2,1)} %all-gather.6.cloned.1.call-done), kind=kOutput, calls=%fused_computation.1 | convolution fusion | flops 1879162880 | bytes 17006592 | tf_op jit(solution)/shard_map/dot_general | solution.py:19
Async XLA Ops:
  7.2 80.5 %all-gather.4.cloned.1.call-start = ((), (), s32[]{:S(2)}) async-start(), calls=%async_computation.1 | async-start | bytes 2162688 | tf_op jit(solution)/shard_map/all_gather | solution.py:8
  7.9 148.7 %all-gather.8.cloned.1.call-start = ((), (), s32[]{:S(2)}) async-start(), calls=%async_computation.3 | async-start | bytes 3899392 | tf_op jit(solution)/shard_map/all_gather | solution.py:11
  8.6 275.4 %all-gather.6.cloned.1.call-start = ((), (), s32[]{:S(2)}) async-start(), calls=%async_computation.2 | async-start | bytes 15597568 | tf_op jit(solution)/shard_map/all_gather | solution.py:21
  127.9 156.1 %copy-start = (bf16[128,16,512]{0,2,1:T(8,128)(2,1)S(1)}, bf16[128,16,512]{0,2,1:T(8,128)(2,1)}, u32[]{:S(2)}) copy-start(bf16[128,16,512]{0,2,1:T(8,128)(2,1)} %copy.5) | copy-start | bytes 6291460
Sparse Core Ops, SparseCore 0:
  10.1 77.5 all-gather.3
  90.7 65.8 all-gather.7
  159.6 124.4 all-gather.5
where the time goes:
time: 301 us
  waiting for transfers between devices  231 us (77%)
  blocking collectives  37.9 us (13%)
  matrix products  16.3 us (5%)
  between operations  13.7 us (5%)
    all_gather x1, waiting for transfers between devices, on_device(): lax.all_gather(weight, 'row', axis=1, tiled=True)  122 us
    all_gather x1, waiting for transfers between devices, on_device(): gathered = lax.all_gather(out_grad, 'col', axis=0, tiled=True)  78.3 us
    all_to_all x1, blocking collectives, on_device(): lax.all_to_all(gathered, 'row', split_axis=0, concat_axis=1, tiled=True)  37.9 us
    all_gather x1, waiting for transfers between devices, on_device(): lax.all_gather(hidden, 'row', axis=0, tiled=True)  28.6 us
    dot_general x1, matrix products, on_device(): lax.dot_general(cotangent, lax.all_gather(weight, 'row', axis=1, tiled=Tr...  10.6 us
  transfers between devices with their start and end apart: 3, of which 3 were waited for; matrix products, arithmetic and copies ran while one was open for 3% of the time, Pallas kernels for 0%

commit v1 on v0

--- a/solution.py
+++ b/solution.py
@@ -8,7 +8,9 @@
     gathered = lax.all_gather(out_grad, "col", axis=0, tiled=True)
     cotangent = gathered
     weight_sum = lax.dot_general(
-        lax.all_gather(hidden, "row", axis=0, tiled=True),
+        jnp.concatenate(
+            lax.all_to_all(jnp.stack([hidden] * lax.axis_size("row")), "row", 0, 0), axis=0
+        ),
         cotangent,
         (((0,), (0,)), ((), ())),
         preferred_element_type=jnp.float32,

time: 301 us -> 239 us (0.79)
  waiting for transfers between devices: 231 us -> 147 us
  blocking collectives: 37.9 us -> 50.3 us
  starting transfers between devices: 0.11 us -> 6.76 us
    all_gather x1, waiting for transfers between devices: 78.3 us -> 27.1 us  [on_device(): gathered = lax.all_gather(out_grad, 'col', axis=0, tiled=True)]
    all_gather x1, waiting for transfers between devices: 122 us -> 86.1 us  [on_device(): lax.all_gather(weight, 'row', axis=1, tiled=True)]
    all_to_all x0 -> x1, waiting for transfers between devices: none -> 32 us  [on_device(): lax.all_to_all(gathered, 'row', split_axis=0, concat_axis=1, tiled=True)]
    all_gather x1 -> x0, waiting for transfers between devices: 28.6 us -> none  [on_device(): lax.all_gather(hidden, 'row', axis=0, tiled=True)]
    all_to_all x1, blocking collectives: 37.9 us -> 50.3 us  [on_device(): lax.all_to_all(jnp.stack([hidden] * lax.axis_size('row')), 'row', 0, 0)]
    all_to_all x0 -> x1, starting transfers between devices: none -> 6.69 us  [on_device(): lax.all_to_all(gathered, 'row', split_axis=0, concat_axis=1, tiled=True)]
  transfers between devices with their start and end apart: 3 -> 3, of which waited for: 3 -> 3; matrix products, arithmetic and copies ran while one was open for 3% -> 4% of each run, Pallas kernels for 0% -> 0%
where the time goes in v1:
time: 239 us; the launch traced here: 238 us
  waiting for transfers between devices  147 us (62%)
  blocking collectives  50.3 us (21%)
  matrix products  16.9 us (7%)
  between operations  14.1 us (6%)
  starting transfers between devices  6.76 us (3%)
  local copies, waits for them, and re-layouts  3.81 us (2%)
    all_gather x1, waiting for transfers between devices, on_device(): lax.all_gather(weight, 'row', axis=1, tiled=True)  86.1 us
    all_to_all x1, blocking collectives, on_device(): lax.all_to_all(jnp.stack([hidden] * lax.axis_size('row')), 'row', 0, 0)  50.3 us
    all_to_all x1, waiting for transfers between devices, on_device(): lax.all_to_all(gathered, 'row', split_axis=0, concat_axis=1, tiled=True)  32 us
    all_gather x1, waiting for transfers between devices, on_device(): gathered = lax.all_gather(out_grad, 'col', axis=0, tiled=True)  27.1 us
    dot_general x1, matrix products, on_device(): lax.dot_general(cotangent, lax.all_gather(weight, 'row', axis=1, tiled=Tr...  11.2 us
    all_to_all x1, starting transfers between devices, on_device(): lax.all_to_all(gathered, 'row', split_axis=0, concat_axis=1, tiled=True)  6.69 us
    dot_general x1, matrix products, on_device(): lax.dot_general(jnp.concatenate(lax.all_to_all(jnp.stack([hidden] * lax.a...  5.72 us
  transfers between devices with their start and end apart: 3, of which 3 were waited for; matrix products, arithmetic and copies ran while one was open for 4% of the time, Pallas kernels for 0%

profile of v1, /device:TPU:1, one launch (start us, length us, event | category | flops | bytes accessed | tf_op | source)
XLA Modules:
  0.0 238.4 jit_solution(16517772892827461739)
XLA Ops:
  7.2 0.0 all-gather.3.cloned.1.call-start
  7.2 0.7 all-gather.3.cloned.1.call-update
  7.9 0.0 all-gather.5.cloned.1.call-start
  7.9 0.7 all-gather.5.cloned.1.call-update
  8.6 1.4 stack.2
  10.1 50.3 %all_to_all.24 = bf16[16,128,896]{2,1,0:T(8,128)(2,1)} all-to-all(bf16[16,128,896]{2,1,0:T(8,128)(2,1)S(1)} %stack.2), channel_id=1, replica_groups=mesh['row'=16,'col'=32] {'row'}, dimensions={0} | all-to-all | bytes 7340032 | tf_op jit(solution)/shard_map/all_to_all | solution.py:12
  60.4 27.1 %all-gather.3.cloned.1.call-done = bf16[2048,512]{1,0:T(8,128)(2,1)} async-done(((bf16[64,512]{1,0:T(8,128)(2,1)}), bf16[2048,512]{1,0:T(8,128)(2,1)}) %all-gather.3.cloned.1.call-update) | async-done | bytes 2097168 | tf_op jit(solution)/shard_map/all_gather | solution.py:8
  87.4 6.7 %all-to-all-start = ((bf16[16,128,512]{2,1,0:T(8,128)(2,1)}), bf16[16,128,512]{2,1,0:T(8,128)(2,1)S(1)}, u32[]{:S(2)}, u32[]{:S(2)}) async-start(bf16[16,128,512]{2,1,0:T(8,128)(2,1)} %bitcast.11), calls=%async_computation | async-start | bytes 4194304 | tf_op jit(solution)/shard_map/all_to_all | solution.py:19
  94.1 5.7 %convolution_convert_fusion = bf16[896,512]{1,0:T(8,128)(2,1)} fusion(bf16[2048,896]{1,0:T(8,128)(2,1)} %bitcast.10, bf16[2048,512]{1,0:T(8,128)(2,1)} %all-gather.3.cloned.1.call-done), kind=kOutput, calls=%fused_computation | convolution fusion | flops 1879506944 | bytes 6684672 | tf_op jit(solution)/shard_map/dot_general | solution.py:10
  99.9 32.0 %all-to-all-done = bf16[16,128,512]{2,1,0:T(8,128)(2,1)S(1)} async-done(((bf16[16,128,512]{2,1,0:T(8,128)(2,1)}), bf16[16,128,512]{2,1,0:T(8,128)(2,1)S(1)}, u32[]{:S(2)}, u32[]{:S(2)}) %all-to-all-start) | async-done | bytes 2097184 | tf_op jit(solution)/shard_map/all_to_all | solution.py:19
  131.9 2.4 copy.5
  134.2 86.1 %all-gather.5.cloned.1.call-done = bf16[896,8192]{1,0:T(8,128)(2,1)} async-done(((bf16[896,512]{1,0:T(8,128)(2,1)}), bf16[896,8192]{1,0:T(8,128)(2,1)}) %all-gather.5.cloned.1.call-update) | async-done | bytes 14680080 | tf_op jit(solution)/shard_map/all_gather | solution.py:23
  220.3 11.2 %convolution_convert_fusion.1 = bf16[128,896]{1,0:T(8,128)(2,1)} fusion(bf16[128,8192]{0,1:T(8,128)(2,1)} %bitcast.9, bf16[896,8192]{1,0:T(8,128)(2,1)} %all-gather.5.cloned.1.call-done), kind=kOutput, calls=%fused_computation.1 | convolution fusion | flops 1879162880 | bytes 17006592 | tf_op jit(solution)/shard_map/dot_general | solution.py:21
Async XLA Ops:
  7.2 80.3 %all-gather.3.cloned.1.call-start = ((), (), s32[]{:S(2)}) async-start(), calls=%async_computation.2 | async-start | bytes 2162688 | tf_op jit(solution)/shard_map/all_gather | solution.py:8
  7.9 212.4 %all-gather.5.cloned.1.call-start = ((), (), s32[]{:S(2)}) async-start(), calls=%async_computation.3 | async-start | bytes 15597568 | tf_op jit(solution)/shard_map/all_gather | solution.py:23
  87.4 44.4 %all-to-all-start = ((bf16[16,128,512]{2,1,0:T(8,128)(2,1)}), bf16[16,128,512]{2,1,0:T(8,128)(2,1)S(1)}, u32[]{:S(2)}, u32[]{:S(2)}) async-start(bf16[16,128,512]{2,1,0:T(8,128)(2,1)} %bitcast.11), calls=%async_computation | async-start | bytes 4194304 | tf_op jit(solution)/shard_map/all_to_all | solution.py:19
Sparse Core Ops, SparseCore 0:
  10.1 77.2 all-gather.2
  90.4 129.8 all-gather.4
